TPU v7x, 256 devices: a whole 4x4x8 slice. The times are simulated.
256 devices in a mesh: section: 8 (over x, y_hi), dp: 32 (over y_lo, z, core).
Axes of the slice: x: 4, y: 4 (y_hi: 2, y_lo: 2; y = y_hi * 2 + y_lo), z: 8, core: 2. Of those that a mesh axis runs over, the one named last changes fastest.
Arguments:
- latent: bfloat16 [8192, 1536], P('dp'), may hold values from -6 to 6
- target: bfloat16 [8192, 1536], P('dp'), may hold values from -6 to 6
- camera_of_token: int32 [8192], P('dp'), may hold values from 0 to 5
- timestep_indices: int32 [2], replicated, may hold values from 0 to 49
- camera_embedding_table: bfloat16 [6, 1536], replicated, may hold values from -3 to 3
- timestep_embedding_table: bfloat16 [50, 1536], replicated, may hold values from -2.5 to 2.5
- layer_norm_gain: float32 [8, 1536], P('section'), may hold values from 0.25 to 1.75
- frozen_weight: bfloat16 [8, 1536, 1536], P('section', 'dp'), may hold values from -0.15625 to 0.15625
- adapter_down_weight: bfloat16 [8, 64, 1536], P('section'), may hold values from -0.15625 to 0.15625
- adapter_up_weight: bfloat16 [8, 64, 1536], P('section'), may hold values from -0.75 to 0.75
Outputs:
- grad_down: float32 [8, 64, 1536], P('section', None, 'dp')
- grad_up: float32 [8, 64, 1536], P('section', None, 'dp')
Inputs may be any that keep to these rules, and one draw needn't show every extreme that they name: `timestep_indices`: indices of rows of timestep_embedding_table.
All inputs are finite; a program needn't handle non-finite values.
Results may differ from a plain program's by a relative error of at most 0.024.
Values may be sent and summed in bfloat16 or wider, within the bound.
No kernel may reach another device: no remote copies, remote signals or barrier semaphores. Data moves between devices by JAX's collectives and lax.ppermute only.
A program may use at most 64 MiB of HBM per device.

v0:
```python
import math
import jax
import jax.numpy as jnp
from jax import lax
from jax.sharding import PartitionSpec as P

MICRO = 4
BLEND = 0.5
ADAPTER_SCALE = 0.5
EPSILON = 1e-06


def from_behind(block, axis, distance):
    devices = range(lax.axis_size(axis))
    route = [((i - distance) % len(devices), i) for i in devices]
    return lax.ppermute(block, axis, route)


def in_one_piece(arrays, axis, dim, along):
    widths = [a.shape[along] for a in arrays]
    both = jnp.concatenate(arrays, axis=along)
    out = lax.psum_scatter(both, axis, scatter_dimension=dim, tiled=True)
    return tuple(jnp.split(out, [sum(widths[:k]) for k in range(1, len(widths))], axis=along))


def forward_layer_pass(
    hidden_state, layer_weight, down_weight_rows, up_weight_rows, gain_row, modulate_row
):
    hidden_float = hidden_state.astype(jnp.float32)
    inverse_rms = lax.rsqrt(jnp.mean(hidden_float * hidden_float, axis=-1, keepdims=True) + EPSILON)
    normalized_hidden = (hidden_float * inverse_rms * (gain_row * modulate_row)).astype(
        jnp.bfloat16
    )
    low_rank_hidden = lax.dot_general(
        normalized_hidden,
        down_weight_rows,
        (((1,), (1,)), ((), ())),
        preferred_element_type=jnp.float32,
    ).astype(jnp.bfloat16)
    preactivation = jnp.dot(
        normalized_hidden, layer_weight, preferred_element_type=jnp.float32
    ) + ADAPTER_SCALE * jnp.dot(low_rank_hidden, up_weight_rows, preferred_element_type=jnp.float32)
    output = (hidden_float + jax.nn.silu(preactivation)).astype(jnp.bfloat16)
    return (output, normalized_hidden, low_rank_hidden, preactivation)


def backward_layer_pass(
    hidden_state,
    normalized_hidden,
    low_rank_hidden,
    preactivation,
    output_gradient,
    layer_weight,
    down_weight_rows,
    up_weight_rows,
    gain_row,
    modulate_row,
):
    sigmoid_value = jax.nn.sigmoid(preactivation)
    preactivation_gradient = (
        output_gradient * sigmoid_value * (1.0 + preactivation * (1.0 - sigmoid_value))
    ).astype(jnp.bfloat16)
    low_rank_gradient = (
        ADAPTER_SCALE
        * lax.dot_general(
            preactivation_gradient,
            up_weight_rows,
            (((1,), (1,)), ((), ())),
            preferred_element_type=jnp.float32,
        )
    ).astype(jnp.bfloat16)
    norm_grad = lax.dot_general(
        preactivation_gradient,
        layer_weight,
        (((1,), (1,)), ((), ())),
        preferred_element_type=jnp.float32,
    ) + jnp.dot(low_rank_gradient, down_weight_rows, preferred_element_type=jnp.float32)
    up_gradient_term = ADAPTER_SCALE * lax.dot_general(
        low_rank_hidden,
        preactivation_gradient,
        (((0,), (0,)), ((), ())),
        preferred_element_type=jnp.float32,
    )
    down_gradient_term = lax.dot_general(
        low_rank_gradient,
        normalized_hidden,
        (((0,), (0,)), ((), ())),
        preferred_element_type=jnp.float32,
    )
    hidden_float = hidden_state.astype(jnp.float32)
    inverse_rms = lax.rsqrt(jnp.mean(hidden_float * hidden_float, axis=-1, keepdims=True) + EPSILON)
    scaled = hidden_float * inverse_rms
    scaled_grad = norm_grad * (gain_row * modulate_row)
    hidden_gradient = output_gradient + inverse_rms * (
        scaled_grad - scaled * jnp.mean(scaled_grad * scaled, axis=-1, keepdims=True)
    )
    return (hidden_gradient, down_gradient_term, up_gradient_term)


def pick_block(store, first_index, second_index):
    anchor = jnp.zeros((), jnp.int32)
    starts = (first_index, second_index) + (anchor,) * (store.ndim - 2)
    piece = lax.dynamic_slice(store, starts, (1, 1) + store.shape[2:])
    return piece[0, 0]


def place_block(store, value, first_index, second_index):
    anchor = jnp.zeros((), jnp.int32)
    starts = (first_index, second_index) + (anchor,) * (store.ndim - 2)
    return lax.dynamic_update_slice(store, value[None, None], starts)


def local(
    latent,
    target,
    camera_of_token,
    timestep_indices,
    camera_embedding_table,
    timestep_embedding_table,
    layer_norm_gain,
    frozen_weight,
    adapter_down_weight,
    adapter_up_weight,
):
    sections = lax.axis_size("section")
    position = lax.axis_index("section")
    layer_weight = lax.all_gather(frozen_weight[0], "dp", axis=0, tiled=True)
    down_weight_rows = adapter_down_weight[0]
    up_weight_rows = adapter_up_weight[0]
    gain_row = layer_norm_gain[0]
    feature_width = latent.shape[1]
    rank_width = down_weight_rows.shape[0]
    scale_factor = 1.0 / math.sqrt(latent.shape[0] * lax.axis_size("dp"))
    camera_rows = jnp.dot(
        jax.nn.one_hot(camera_of_token, camera_embedding_table.shape[0], dtype=jnp.bfloat16),
        camera_embedding_table,
        preferred_element_type=jnp.float32,
    )
    timestep_modulation = 1.0 + jnp.dot(
        jax.nn.one_hot(timestep_indices, timestep_embedding_table.shape[0], dtype=jnp.bfloat16),
        timestep_embedding_table,
        preferred_element_type=jnp.float32,
    )
    block_count = MICRO
    block_rows = latent.shape[0] // block_count
    latent_blocks = latent.reshape(block_count, block_rows, feature_width)
    target_blocks = target.reshape(block_count, block_rows, feature_width)
    camera_blocks = camera_rows.reshape(block_count, block_rows, feature_width)
    is_first = position == 0
    is_last = position == sections - 1
    tick_total = 2 * sections + block_count - 1
    zero_index = jnp.zeros((), jnp.int32)

    def forward_tick(tick_index, carry):
        offset = tick_index - position
        round_index = (offset >= sections).astype(jnp.int32)
        block_index = offset - round_index * sections
        active = (offset >= 0) & (block_index < block_count)
        safe_block = jnp.clip(block_index, 0, block_count - 1)

        def forward_compute(current):
            (
                received,
                hidden_store,
                normed_store,
                low_store,
                pre_store,
                blend_store,
                adjoint_store,
            ) = current
            latent_block = lax.dynamic_index_in_dim(
                latent_blocks, safe_block, 0, keepdims=False
            ).astype(jnp.float32)
            camera_block = lax.dynamic_index_in_dim(camera_blocks, safe_block, 0, keepdims=False)
            target_block = lax.dynamic_index_in_dim(
                target_blocks, safe_block, 0, keepdims=False
            ).astype(jnp.float32)
            starting = jnp.where(round_index == 0, latent_block, received.astype(jnp.float32))
            first_hidden = (starting + camera_block).astype(jnp.bfloat16)
            hidden_state = jnp.where(is_first, first_hidden, received)
            modulate_row = jnp.where(
                round_index == 0, timestep_modulation[0], timestep_modulation[1]
            )
            output, normalized_hidden, low_rank_hidden, preactivation = forward_layer_pass(
                hidden_state, layer_weight, down_weight_rows, up_weight_rows, gain_row, modulate_row
            )
            hidden_store = place_block(hidden_store, hidden_state, round_index, safe_block)
            normed_store = place_block(normed_store, normalized_hidden, round_index, safe_block)
            low_store = place_block(low_store, low_rank_hidden, round_index, safe_block)
            pre_store = place_block(pre_store, preactivation, round_index, safe_block)
            previous_blend = lax.dynamic_index_in_dim(blend_store, safe_block, 0, keepdims=False)
            previous = jnp.where(round_index == 0, latent_block, previous_blend.astype(jnp.float32))
            blended = BLEND * (previous + output.astype(jnp.float32))
            blend_rounded = blended.astype(jnp.bfloat16)
            keep_blend = jnp.where(round_index == 0, blend_rounded, previous_blend)
            blend_store = lax.dynamic_update_slice(
                blend_store, keep_blend[None], (safe_block, zero_index, zero_index)
            )
            squashed = jnp.tanh(blended)
            adjoint = target_block * (1.0 - squashed * squashed) * scale_factor
            previous_adjoint = lax.dynamic_index_in_dim(
                adjoint_store, safe_block, 0, keepdims=False
            )
            keep_adjoint = jnp.where(round_index == 1, adjoint, previous_adjoint)
            adjoint_store = lax.dynamic_update_slice(
                adjoint_store, keep_adjoint[None], (safe_block, zero_index, zero_index)
            )
            outgoing = jnp.where(is_last, blend_rounded, output)
            return (
                outgoing,
                (hidden_store, normed_store, low_store, pre_store, blend_store, adjoint_store),
            )

        def forward_skip_block(current):
            return (jnp.zeros_like(current[0]), tuple(current[1:]))

        outgoing, stores = lax.cond(active, forward_compute, forward_skip_block, carry)
        incoming = from_behind(outgoing, "section", 1)
        return (incoming,) + tuple(stores)

    forward_start = (
        jnp.zeros((block_rows, feature_width), jnp.bfloat16),
        jnp.zeros((2, block_count, block_rows, feature_width), jnp.bfloat16),
        jnp.zeros((2, block_count, block_rows, feature_width), jnp.bfloat16),
        jnp.zeros((2, block_count, block_rows, rank_width), jnp.bfloat16),
        jnp.zeros((2, block_count, block_rows, feature_width), jnp.float32),
        jnp.zeros((block_count, block_rows, feature_width), jnp.bfloat16),
        jnp.zeros((block_count, block_rows, feature_width), jnp.float32),
    )
    forward_end = lax.fori_loop(0, tick_total, forward_tick, forward_start)
    hidden_store, normed_store, low_store, pre_store, blend_store, adjoint_store = forward_end[1:]
    back_position = sections - 1 - position

    def backward_tick(tick_index, carry):
        offset = tick_index - back_position
        round_back = (offset >= sections).astype(jnp.int32)
        block_index = offset - round_back * sections
        active = (offset >= 0) & (block_index < block_count)
        safe_block = jnp.clip(block_index, 0, block_count - 1)
        forward_round = 1 - round_back

        def backward_compute(current):
            received, down_sum, up_sum = current
            adjoint_block = lax.dynamic_index_in_dim(adjoint_store, safe_block, 0, keepdims=False)
            received_float = received.astype(jnp.float32)
            last_cotangent = jnp.where(
                round_back == 0,
                BLEND * adjoint_block,
                BLEND * (BLEND * adjoint_block + received_float),
            )
            output_gradient = jnp.where(is_last, last_cotangent, received_float)
            hidden_state = pick_block(hidden_store, forward_round, safe_block)
            normalized_hidden = pick_block(normed_store, forward_round, safe_block)
            low_rank_hidden = pick_block(low_store, forward_round, safe_block)
            preactivation = pick_block(pre_store, forward_round, safe_block)
            modulate_row = jnp.where(
                forward_round == 0, timestep_modulation[0], timestep_modulation[1]
            )
            hidden_gradient, down_gradient_term, up_gradient_term = backward_layer_pass(
                hidden_state,
                normalized_hidden,
                low_rank_hidden,
                preactivation,
                output_gradient,
                layer_weight,
                down_weight_rows,
                up_weight_rows,
                gain_row,
                modulate_row,
            )
            return (
                hidden_gradient.astype(jnp.bfloat16),
                down_sum + down_gradient_term,
                up_sum + up_gradient_term,
            )

        def backward_skip_block(current):
            return (jnp.zeros_like(current[0]), current[1], current[2])

        outgoing, down_sum, up_sum = lax.cond(active, backward_compute, backward_skip_block, carry)
        incoming = from_behind(outgoing, "section", -1)
        return (incoming, down_sum, up_sum)

    backward_start = (
        jnp.zeros((block_rows, feature_width), jnp.bfloat16),
        jnp.zeros((rank_width, feature_width), jnp.float32),
        jnp.zeros((rank_width, feature_width), jnp.float32),
    )
    backward_end = lax.fori_loop(0, tick_total, backward_tick, backward_start)
    down_part, up_part = in_one_piece((backward_end[1], backward_end[2]), "dp", 1, 0)
    return (down_part[None], up_part[None])


def solution(mesh):
    in_specs = (
        P("dp", None),
        P("dp", None),
        P("dp"),
        P(),
        P(),
        P(),
        P("section", None),
        P("section", "dp", None),
        P("section", None, None),
        P("section", None, None),
    )
    out_specs = (P("section", None, "dp"), P("section", None, "dp"))
    return jax.shard_map(local, mesh=mesh, in_specs=in_specs, out_specs=out_specs, check_vma=False)
```

profile of v0, /device:TPU:6, one launch (start us, length us, event | category | flops | bytes accessed | tf_op | source)
XLA Modules:
  0.0 969.5 jit_solution(15846906296157261650)
XLA Ops:
  12.0 68.9 %all-gather.3.cloned.1.call-done = bf16[1,1536,1536]{2,1,0:T(8,128)(2,1)} async-done(((bf16[1,48,1536]{2,1,0:T(8,128)(2,1)}), bf16[1,1536,1536]{2,1,0:T(8,128)(2,1)}) %all-gather.3.cloned.1.call-update) | async-done | bytes 4718608 | tf_op jit(solution)/shard_map/all_gather | solution.py:127
  86.8 397.1 %while.42 = (s32[]{:T(128)}, bf16[64,1536]{1,0:T(8,128)(2,1)}, bf16[2,4,64,1536]{3,2,1,0:T(8,128)(2,1)S(1)}, bf16[2,4,64,1536]{3,2,1,0:T(8,128)(2,1)}, bf16[2,4,...) while((s32[]{:T(128)}, bf16[64,1536]{1,0:T(8,128)(2,1)}, ...), condition=%wide.region_4.5_spmd, body=%wide.region_0.4_spmd.sunk | while | flops 332176448 | bytes 21725468 | solution.py:230
  115.6 19.0 %collective-permute-start = (bf16[64,1536]{1,0:T(8,128)(2,1)}, bf16[64,1536]{1,0:T(8,128)(2,1)S(1)}, u32[]{:S(2)}, u32[]{:S(2)}) collective-permute-start(bf16[64,1536]{1,0:T(8,128)(2,1)} %get-tuple-element.1111), channel_id=1, source_target_pairs={{224,0},{0,32},{32,64},{64,96},{96,128},{128,160},{160,192},{192,2... | collective-permute-start | bytes 589832 | tf_op jit(solution)/shard_map/while/body/eval_jaxpr/ppermute | solution.py:16
  139.5 19.0 %collective-permute-start = (bf16[64,1536]{1,0:T(8,128)(2,1)}, bf16[64,1536]{1,0:T(8,128)(2,1)S(1)}, u32[]{:S(2)}, u32[]{:S(2)}) collective-permute-start(bf16[64,1536]{1,0:T(8,128)(2,1)} %get-tuple-element.1111), channel_id=1, source_target_pairs={{224,0},{0,32},{32,64},{64,96},{96,128},{128,160},{160,192},{192,2... | collective-permute-start | bytes 589832 | tf_op jit(solution)/shard_map/while/body/eval_jaxpr/ppermute | solution.py:16
  163.4 19.0 %collective-permute-start = (bf16[64,1536]{1,0:T(8,128)(2,1)}, bf16[64,1536]{1,0:T(8,128)(2,1)S(1)}, u32[]{:S(2)}, u32[]{:S(2)}) collective-permute-start(bf16[64,1536]{1,0:T(8,128)(2,1)} %get-tuple-element.1111), channel_id=1, source_target_pairs={{224,0},{0,32},{32,64},{64,96},{96,128},{128,160},{160,192},{192,2... | collective-permute-start | bytes 589832 | tf_op jit(solution)/shard_map/while/body/eval_jaxpr/ppermute | solution.py:16
  193.3 16.5 %collective-permute-done = bf16[64,1536]{1,0:T(8,128)(2,1)S(1)} collective-permute-done((bf16[64,1536]{1,0:T(8,128)(2,1)}, bf16[64,1536]{1,0:T(8,128)(2,1)S(1)}, u32[]{:S(2)}, u32[]{:S(2)}) %collective-permute-start) | collective-permute-done | bytes 196640 | tf_op jit(solution)/shard_map/while/body/eval_jaxpr/ppermute | solution.py:16
  210.5 13.7 %conditional.4 = (bf16[64,1536]{1,0:T(8,128)(2,1)}, bf16[2,4,64,1536]{3,2,1,0:T(8,128)(2,1)S(1)}, bf16[2,4,64,1536]{3,2,1,0:T(8,128)(2,1)}, bf16[2,4,64,64]{3,2,...) conditional(s32[]{:T(128)} %convert_element_type.177, ...), branch_computations={%region_1.1_spmd, %region_2.3_spmd} | conditional | flops 332176448 | bytes 20152056 | solution.py:217
  233.4 13.7 %conditional.4 = (bf16[64,1536]{1,0:T(8,128)(2,1)}, bf16[2,4,64,1536]{3,2,1,0:T(8,128)(2,1)S(1)}, bf16[2,4,64,1536]{3,2,1,0:T(8,128)(2,1)}, bf16[2,4,64,64]{3,2,...) conditional(s32[]{:T(128)} %convert_element_type.177, ...), branch_computations={%region_1.1_spmd, %region_2.3_spmd} | conditional | flops 332176448 | bytes 20152056 | solution.py:217
  256.7 13.7 %conditional.4 = (bf16[64,1536]{1,0:T(8,128)(2,1)}, bf16[2,4,64,1536]{3,2,1,0:T(8,128)(2,1)S(1)}, bf16[2,4,64,1536]{3,2,1,0:T(8,128)(2,1)}, bf16[2,4,64,64]{3,2,...) conditional(s32[]{:T(128)} %convert_element_type.177, ...), branch_computations={%region_1.1_spmd, %region_2.3_spmd} | conditional | flops 332176448 | bytes 20152056 | solution.py:217
  280.5 13.7 %conditional.4 = (bf16[64,1536]{1,0:T(8,128)(2,1)}, bf16[2,4,64,1536]{3,2,1,0:T(8,128)(2,1)S(1)}, bf16[2,4,64,1536]{3,2,1,0:T(8,128)(2,1)}, bf16[2,4,64,64]{3,2,...) conditional(s32[]{:T(128)} %convert_element_type.177, ...), branch_computations={%region_1.1_spmd, %region_2.3_spmd} | conditional | flops 332176448 | bytes 20152056 | solution.py:217
  330.6 17.2 %collective-permute-start = (bf16[64,1536]{1,0:T(8,128)(2,1)}, bf16[64,1536]{1,0:T(8,128)(2,1)S(1)}, u32[]{:S(2)}, u32[]{:S(2)}) collective-permute-start(bf16[64,1536]{1,0:T(8,128)(2,1)} %get-tuple-element.1111), channel_id=1, source_target_pairs={{224,0},{0,32},{32,64},{64,96},{96,128},{128,160},{160,192},{192,2... | collective-permute-start | bytes 589832 | tf_op jit(solution)/shard_map/while/body/eval_jaxpr/ppermute | solution.py:16
  358.7 13.3 %collective-permute-done = bf16[64,1536]{1,0:T(8,128)(2,1)S(1)} collective-permute-done((bf16[64,1536]{1,0:T(8,128)(2,1)}, bf16[64,1536]{1,0:T(8,128)(2,1)S(1)}, u32[]{:S(2)}, u32[]{:S(2)}) %collective-permute-start) | collective-permute-done | bytes 196640 | tf_op jit(solution)/shard_map/while/body/eval_jaxpr/ppermute | solution.py:16
  372.7 13.7 %conditional.4 = (bf16[64,1536]{1,0:T(8,128)(2,1)}, bf16[2,4,64,1536]{3,2,1,0:T(8,128)(2,1)S(1)}, bf16[2,4,64,1536]{3,2,1,0:T(8,128)(2,1)}, bf16[2,4,64,64]{3,2,...) conditional(s32[]{:T(128)} %convert_element_type.177, ...), branch_computations={%region_1.1_spmd, %region_2.3_spmd} | conditional | flops 332176448 | bytes 20152056 | solution.py:217
  396.6 13.7 %conditional.4 = (bf16[64,1536]{1,0:T(8,128)(2,1)}, bf16[2,4,64,1536]{3,2,1,0:T(8,128)(2,1)S(1)}, bf16[2,4,64,1536]{3,2,1,0:T(8,128)(2,1)}, bf16[2,4,64,64]{3,2,...) conditional(s32[]{:T(128)} %convert_element_type.177, ...), branch_computations={%region_1.1_spmd, %region_2.3_spmd} | conditional | flops 332176448 | bytes 20152056 | solution.py:217
  420.5 13.7 %conditional.4 = (bf16[64,1536]{1,0:T(8,128)(2,1)}, bf16[2,4,64,1536]{3,2,1,0:T(8,128)(2,1)S(1)}, bf16[2,4,64,1536]{3,2,1,0:T(8,128)(2,1)}, bf16[2,4,64,64]{3,2,...) conditional(s32[]{:T(128)} %convert_element_type.177, ...), branch_computations={%region_1.1_spmd, %region_2.3_spmd} | conditional | flops 332176448 | bytes 20152056 | solution.py:217
  444.3 13.7 %conditional.4 = (bf16[64,1536]{1,0:T(8,128)(2,1)}, bf16[2,4,64,1536]{3,2,1,0:T(8,128)(2,1)S(1)}, bf16[2,4,64,1536]{3,2,1,0:T(8,128)(2,1)}, bf16[2,4,64,64]{3,2,...) conditional(s32[]{:T(128)} %convert_element_type.177, ...), branch_computations={%region_1.1_spmd, %region_2.3_spmd} | conditional | flops 332176448 | bytes 20152056 | solution.py:217
  467.6 12.1 %collective-permute-start = (bf16[64,1536]{1,0:T(8,128)(2,1)}, bf16[64,1536]{1,0:T(8,128)(2,1)S(1)}, u32[]{:S(2)}, u32[]{:S(2)}) collective-permute-start(bf16[64,1536]{1,0:T(8,128)(2,1)} %get-tuple-element.1111), channel_id=1, source_target_pairs={{224,0},{0,32},{32,64},{64,96},{96,128},{128,160},{160,192},{192,2... | collective-permute-start | bytes 589832 | tf_op jit(solution)/shard_map/while/body/eval_jaxpr/ppermute | solution.py:16
  485.2 342.2 %while.43 = (s32[]{:T(128)}, bf16[64,1536]{1,0:T(8,128)(2,1)S(1)}, f32[64,1536]{1,0:T(8,128)S(1)}, f32[64,1536]{1,0:T(8,128)S(1)}, s32[]{:T(128)}, /*index=5*/pr...) while((s32[]{:T(128)}, bf16[64,1536]{1,0:T(8,128)(2,1)S(1)}, ...), condition=%wide.region_10.11_spmd, body=%wide.region_5.10_spmd.sunk | while | flops 356265024 | bytes 13259635 | solution.py:289
  485.9 18.9 %collective-permute-done.1 = bf16[64,1536]{1,0:T(8,128)(2,1)S(1)} collective-permute-done((bf16[64,1536]{1,0:T(8,128)(2,1)}, bf16[64,1536]{1,0:T(8,128)(2,1)S(1)}, u32[]{:S(2)}, u32[]{:S(2)}) %collective-permute-start.1) | collective-permute-done | bytes 196640 | tf_op jit(solution)/shard_map/while/body/eval_jaxpr/ppermute | solution.py:16
  504.9 11.8 %conditional.5 = (bf16[64,1536]{1,0:T(8,128)(2,1)}, f32[64,1536]{1,0:T(8,128)S(1)}, f32[64,1536]{1,0:T(8,128)S(1)}) conditional(s32[]{:T(128)} %convert_element_type.179, (f32[64,1536]{1,0:T(8,128)S(1)}, f32[64,1536]{1,0:T(8,128)S(1)}) %tuple.93, (pred[]{:T(512)}, s32[]{:T(128)}, s32[]{:T(128)}, f32[4,64,1536]{2,1,0:T(8,128)S(1)}, ...), branch_computations={%region_6.6_spmd, %region_7.9_spmd} | conditional | flops 356265024 | bytes 12472761 | solution.py:280
  526.4 11.8 %conditional.5 = (bf16[64,1536]{1,0:T(8,128)(2,1)}, f32[64,1536]{1,0:T(8,128)S(1)}, f32[64,1536]{1,0:T(8,128)S(1)}) conditional(s32[]{:T(128)} %convert_element_type.179, (f32[64,1536]{1,0:T(8,128)S(1)}, f32[64,1536]{1,0:T(8,128)S(1)}) %tuple.93, (pred[]{:T(512)}, s32[]{:T(128)}, s32[]{:T(128)}, f32[4,64,1536]{2,1,0:T(8,128)S(1)}, ...), branch_computations={%region_6.6_spmd, %region_7.9_spmd} | conditional | flops 356265024 | bytes 12472761 | solution.py:280
  549.4 11.8 %conditional.5 = (bf16[64,1536]{1,0:T(8,128)(2,1)}, f32[64,1536]{1,0:T(8,128)S(1)}, f32[64,1536]{1,0:T(8,128)S(1)}) conditional(s32[]{:T(128)} %convert_element_type.179, (f32[64,1536]{1,0:T(8,128)S(1)}, f32[64,1536]{1,0:T(8,128)S(1)}) %tuple.93, (pred[]{:T(512)}, s32[]{:T(128)}, s32[]{:T(128)}, f32[4,64,1536]{2,1,0:T(8,128)S(1)}, ...), branch_computations={%region_6.6_spmd, %region_7.9_spmd} | conditional | flops 356265024 | bytes 12472761 | solution.py:280
  571.1 11.8 %conditional.5 = (bf16[64,1536]{1,0:T(8,128)(2,1)}, f32[64,1536]{1,0:T(8,128)S(1)}, f32[64,1536]{1,0:T(8,128)S(1)}) conditional(s32[]{:T(128)} %convert_element_type.179, (f32[64,1536]{1,0:T(8,128)S(1)}, f32[64,1536]{1,0:T(8,128)S(1)}) %tuple.93, (pred[]{:T(512)}, s32[]{:T(128)}, s32[]{:T(128)}, f32[4,64,1536]{2,1,0:T(8,128)S(1)}, ...), branch_computations={%region_6.6_spmd, %region_7.9_spmd} | conditional | flops 356265024 | bytes 12472761 | solution.py:280
  591.0 13.7 %collective-permute-start.1 = (bf16[64,1536]{1,0:T(8,128)(2,1)}, bf16[64,1536]{1,0:T(8,128)(2,1)S(1)}, u32[]{:S(2)}, u32[]{:S(2)}) collective-permute-start(bf16[64,1536]{1,0:T(8,128)(2,1)} %get-tuple-element.1134), channel_id=1, source_target_pairs={{32,0},{64,32},{96,64},{128,96},{160,128},{192,160},{224,192},{0,2... | collective-permute-start | bytes 589832 | tf_op jit(solution)/shard_map/while/body/eval_jaxpr/ppermute | solution.py:16
  637.1 15.8 %collective-permute-done.1 = bf16[64,1536]{1,0:T(8,128)(2,1)S(1)} collective-permute-done((bf16[64,1536]{1,0:T(8,128)(2,1)}, bf16[64,1536]{1,0:T(8,128)(2,1)S(1)}, u32[]{:S(2)}, u32[]{:S(2)}) %collective-permute-start.1) | collective-permute-done | bytes 196640 | tf_op jit(solution)/shard_map/while/body/eval_jaxpr/ppermute | solution.py:16
  653.0 11.8 %conditional.5 = (bf16[64,1536]{1,0:T(8,128)(2,1)}, f32[64,1536]{1,0:T(8,128)S(1)}, f32[64,1536]{1,0:T(8,128)S(1)}) conditional(s32[]{:T(128)} %convert_element_type.179, (f32[64,1536]{1,0:T(8,128)S(1)}, f32[64,1536]{1,0:T(8,128)S(1)}) %tuple.93, (pred[]{:T(512)}, s32[]{:T(128)}, s32[]{:T(128)}, f32[4,64,1536]{2,1,0:T(8,128)S(1)}, ...), branch_computations={%region_6.6_spmd, %region_7.9_spmd} | conditional | flops 356265024 | bytes 12472761 | solution.py:280
  674.7 11.8 %conditional.5 = (bf16[64,1536]{1,0:T(8,128)(2,1)}, f32[64,1536]{1,0:T(8,128)S(1)}, f32[64,1536]{1,0:T(8,128)S(1)}) conditional(s32[]{:T(128)} %convert_element_type.179, (f32[64,1536]{1,0:T(8,128)S(1)}, f32[64,1536]{1,0:T(8,128)S(1)}) %tuple.93, (pred[]{:T(512)}, s32[]{:T(128)}, s32[]{:T(128)}, f32[4,64,1536]{2,1,0:T(8,128)S(1)}, ...), branch_computations={%region_6.6_spmd, %region_7.9_spmd} | conditional | flops 356265024 | bytes 12472761 | solution.py:280
  696.3 11.8 %conditional.5 = (bf16[64,1536]{1,0:T(8,128)(2,1)}, f32[64,1536]{1,0:T(8,128)S(1)}, f32[64,1536]{1,0:T(8,128)S(1)}) conditional(s32[]{:T(128)} %convert_element_type.179, (f32[64,1536]{1,0:T(8,128)S(1)}, f32[64,1536]{1,0:T(8,128)S(1)}) %tuple.93, (pred[]{:T(512)}, s32[]{:T(128)}, s32[]{:T(128)}, f32[4,64,1536]{2,1,0:T(8,128)S(1)}, ...), branch_computations={%region_6.6_spmd, %region_7.9_spmd} | conditional | flops 356265024 | bytes 12472761 | solution.py:280
  718.3 11.8 %conditional.5 = (bf16[64,1536]{1,0:T(8,128)(2,1)}, f32[64,1536]{1,0:T(8,128)S(1)}, f32[64,1536]{1,0:T(8,128)S(1)}) conditional(s32[]{:T(128)} %convert_element_type.179, (f32[64,1536]{1,0:T(8,128)S(1)}, f32[64,1536]{1,0:T(8,128)S(1)}) %tuple.93, (pred[]{:T(512)}, s32[]{:T(128)}, s32[]{:T(128)}, f32[4,64,1536]{2,1,0:T(8,128)S(1)}, ...), branch_computations={%region_6.6_spmd, %region_7.9_spmd} | conditional | flops 356265024 | bytes 12472761 | solution.py:280
  738.3 13.0 %collective-permute-start.1 = (bf16[64,1536]{1,0:T(8,128)(2,1)}, bf16[64,1536]{1,0:T(8,128)(2,1)S(1)}, u32[]{:S(2)}, u32[]{:S(2)}) collective-permute-start(bf16[64,1536]{1,0:T(8,128)(2,1)} %get-tuple-element.1134), channel_id=1, source_target_pairs={{32,0},{64,32},{96,64},{128,96},{160,128},{192,160},{224,192},{0,2... | collective-permute-start | bytes 589832 | tf_op jit(solution)/shard_map/while/body/eval_jaxpr/ppermute | solution.py:16
  808.1 19.4 %collective-permute-done.1 = bf16[64,1536]{1,0:T(8,128)(2,1)S(1)} collective-permute-done((bf16[64,1536]{1,0:T(8,128)(2,1)}, bf16[64,1536]{1,0:T(8,128)(2,1)S(1)}, u32[]{:S(2)}, u32[]{:S(2)}) %collective-permute-start.1) | collective-permute-done | bytes 196640 | tf_op jit(solution)/shard_map/while/body/eval_jaxpr/ppermute | solution.py:16
  829.2 132.0 %reduce-scatter.2.cloned.1.call-done = f32[128,48]{0,1:T(8,128)} async-done(((f32[128,1536]{0,1:T(8,128)}), f32[128,48]{0,1:T(8,128)}) %reduce-scatter.2.cloned.1.call-update) | async-done | bytes 24592 | tf_op jit(solution)/shard_map/reduce_scatter | solution.py:22
  (419 shorter events, 571.5 us)
Async XLA Ops:
  7.2 73.6 %all-gather.3.cloned.1.call-start = ((), (), s32[]{:S(2)}) async-start(), calls=%async_computation.2 | async-start | bytes 4866048 | tf_op jit(solution)/shard_map/all_gather | solution.py:127
  7.9 953.3 %reduce-scatter.2.cloned.1.call-start = ((), (), s32[]{:S(2)}) async-start(), calls=%async_computation.1 | async-start | bytes 811008 | tf_op jit(solution)/shard_map/reduce_scatter | solution.py:22
  87.5 9.7 collective-permute-start
  98.5 15.8 %collective-permute-start = (bf16[64,1536]{1,0:T(8,128)(2,1)}, bf16[64,1536]{1,0:T(8,128)(2,1)S(1)}, u32[]{:S(2)}, u32[]{:S(2)}) collective-permute-start(bf16[64,1536]{1,0:T(8,128)(2,1)} %get-tuple-element.1111), channel_id=1, source_target_pairs={{224,0},{0,32},{32,64},{64,96},{96,128},{128,160},{160,192},{192,2... | collective-permute-start | bytes 589832 | tf_op jit(solution)/shard_map/while/body/eval_jaxpr/ppermute | solution.py:16
  115.6 22.5 %collective-permute-start = (bf16[64,1536]{1,0:T(8,128)(2,1)}, bf16[64,1536]{1,0:T(8,128)(2,1)S(1)}, u32[]{:S(2)}, u32[]{:S(2)}) collective-permute-start(bf16[64,1536]{1,0:T(8,128)(2,1)} %get-tuple-element.1111), channel_id=1, source_target_pairs={{224,0},{0,32},{32,64},{64,96},{96,128},{128,160},{160,192},{192,2... | collective-permute-start | bytes 589832 | tf_op jit(solution)/shard_map/while/body/eval_jaxpr/ppermute | solution.py:16
  139.5 22.5 %collective-permute-start = (bf16[64,1536]{1,0:T(8,128)(2,1)}, bf16[64,1536]{1,0:T(8,128)(2,1)S(1)}, u32[]{:S(2)}, u32[]{:S(2)}) collective-permute-start(bf16[64,1536]{1,0:T(8,128)(2,1)} %get-tuple-element.1111), channel_id=1, source_target_pairs={{224,0},{0,32},{32,64},{64,96},{96,128},{128,160},{160,192},{192,2... | collective-permute-start | bytes 589832 | tf_op jit(solution)/shard_map/while/body/eval_jaxpr/ppermute | solution.py:16
  163.4 22.5 %collective-permute-start = (bf16[64,1536]{1,0:T(8,128)(2,1)}, bf16[64,1536]{1,0:T(8,128)(2,1)S(1)}, u32[]{:S(2)}, u32[]{:S(2)}) collective-permute-start(bf16[64,1536]{1,0:T(8,128)(2,1)} %get-tuple-element.1111), channel_id=1, source_target_pairs={{224,0},{0,32},{32,64},{64,96},{96,128},{128,160},{160,192},{192,2... | collective-permute-start | bytes 589832 | tf_op jit(solution)/shard_map/while/body/eval_jaxpr/ppermute | solution.py:16
  187.3 22.5 %collective-permute-start = (bf16[64,1536]{1,0:T(8,128)(2,1)}, bf16[64,1536]{1,0:T(8,128)(2,1)S(1)}, u32[]{:S(2)}, u32[]{:S(2)}) collective-permute-start(bf16[64,1536]{1,0:T(8,128)(2,1)} %get-tuple-element.1111), channel_id=1, source_target_pairs={{224,0},{0,32},{32,64},{64,96},{96,128},{128,160},{160,192},{192,2... | collective-permute-start | bytes 589832 | tf_op jit(solution)/shard_map/while/body/eval_jaxpr/ppermute | solution.py:16
  270.4 9.5 collective-permute-start
  294.2 10.0 %collective-permute-start = (bf16[64,1536]{1,0:T(8,128)(2,1)}, bf16[64,1536]{1,0:T(8,128)(2,1)S(1)}, u32[]{:S(2)}, u32[]{:S(2)}) collective-permute-start(bf16[64,1536]{1,0:T(8,128)(2,1)} %get-tuple-element.1111), channel_id=1, source_target_pairs={{224,0},{0,32},{32,64},{64,96},{96,128},{128,160},{160,192},{192,2... | collective-permute-start | bytes 589832 | tf_op jit(solution)/shard_map/while/body/eval_jaxpr/ppermute | solution.py:16
  305.7 13.8 %collective-permute-start = (bf16[64,1536]{1,0:T(8,128)(2,1)}, bf16[64,1536]{1,0:T(8,128)(2,1)S(1)}, u32[]{:S(2)}, u32[]{:S(2)}) collective-permute-start(bf16[64,1536]{1,0:T(8,128)(2,1)} %get-tuple-element.1111), channel_id=1, source_target_pairs={{224,0},{0,32},{32,64},{64,96},{96,128},{128,160},{160,192},{192,2... | collective-permute-start | bytes 589832 | tf_op jit(solution)/shard_map/while/body/eval_jaxpr/ppermute | solution.py:16
  330.6 21.5 %collective-permute-start = (bf16[64,1536]{1,0:T(8,128)(2,1)}, bf16[64,1536]{1,0:T(8,128)(2,1)S(1)}, u32[]{:S(2)}, u32[]{:S(2)}) collective-permute-start(bf16[64,1536]{1,0:T(8,128)(2,1)} %get-tuple-element.1111), channel_id=1, source_target_pairs={{224,0},{0,32},{32,64},{64,96},{96,128},{128,160},{160,192},{192,2... | collective-permute-start | bytes 589832 | tf_op jit(solution)/shard_map/while/body/eval_jaxpr/ppermute | solution.py:16
  353.5 18.5 %collective-permute-start = (bf16[64,1536]{1,0:T(8,128)(2,1)}, bf16[64,1536]{1,0:T(8,128)(2,1)S(1)}, u32[]{:S(2)}, u32[]{:S(2)}) collective-permute-start(bf16[64,1536]{1,0:T(8,128)(2,1)} %get-tuple-element.1111), channel_id=1, source_target_pairs={{224,0},{0,32},{32,64},{64,96},{96,128},{128,160},{160,192},{192,2... | collective-permute-start | bytes 589832 | tf_op jit(solution)/shard_map/while/body/eval_jaxpr/ppermute | solution.py:16
  386.3 9.6 collective-permute-start
  410.2 9.5 collective-permute-start
  434.1 9.5 collective-permute-start
  467.6 15.6 %collective-permute-start = (bf16[64,1536]{1,0:T(8,128)(2,1)}, bf16[64,1536]{1,0:T(8,128)(2,1)S(1)}, u32[]{:S(2)}, u32[]{:S(2)}) collective-permute-start(bf16[64,1536]{1,0:T(8,128)(2,1)} %get-tuple-element.1111), channel_id=1, source_target_pairs={{224,0},{0,32},{32,64},{64,96},{96,128},{128,160},{160,192},{192,2... | collective-permute-start | bytes 589832 | tf_op jit(solution)/shard_map/while/body/eval_jaxpr/ppermute | solution.py:16
  485.9 18.9 %collective-permute-start.1 = (bf16[64,1536]{1,0:T(8,128)(2,1)}, bf16[64,1536]{1,0:T(8,128)(2,1)S(1)}, u32[]{:S(2)}, u32[]{:S(2)}) collective-permute-start(bf16[64,1536]{1,0:T(8,128)(2,1)} %get-tuple-element.1134), channel_id=1, source_target_pairs={{32,0},{64,32},{96,64},{128,96},{160,128},{192,160},{224,192},{0,2... | collective-permute-start | bytes 589832 | tf_op jit(solution)/shard_map/while/body/eval_jaxpr/ppermute | solution.py:16
  516.7 9.8 %collective-permute-start.1 = (bf16[64,1536]{1,0:T(8,128)(2,1)}, bf16[64,1536]{1,0:T(8,128)(2,1)S(1)}, u32[]{:S(2)}, u32[]{:S(2)}) collective-permute-start(bf16[64,1536]{1,0:T(8,128)(2,1)} %get-tuple-element.1134), channel_id=1, source_target_pairs={{32,0},{64,32},{96,64},{128,96},{160,128},{192,160},{224,192},{0,2... | collective-permute-start | bytes 589832 | tf_op jit(solution)/shard_map/while/body/eval_jaxpr/ppermute | solution.py:16
  538.2 11.2 %collective-permute-start.1 = (bf16[64,1536]{1,0:T(8,128)(2,1)}, bf16[64,1536]{1,0:T(8,128)(2,1)S(1)}, u32[]{:S(2)}, u32[]{:S(2)}) collective-permute-start(bf16[64,1536]{1,0:T(8,128)(2,1)} %get-tuple-element.1134), channel_id=1, source_target_pairs={{32,0},{64,32},{96,64},{128,96},{160,128},{192,160},{224,192},{0,2... | collective-permute-start | bytes 589832 | tf_op jit(solution)/shard_map/while/body/eval_jaxpr/ppermute | solution.py:16
  561.2 9.9 %collective-permute-start.1 = (bf16[64,1536]{1,0:T(8,128)(2,1)}, bf16[64,1536]{1,0:T(8,128)(2,1)S(1)}, u32[]{:S(2)}, u32[]{:S(2)}) collective-permute-start(bf16[64,1536]{1,0:T(8,128)(2,1)} %get-tuple-element.1134), channel_id=1, source_target_pairs={{32,0},{64,32},{96,64},{128,96},{160,128},{192,160},{224,192},{0,2... | collective-permute-start | bytes 589832 | tf_op jit(solution)/shard_map/while/body/eval_jaxpr/ppermute | solution.py:16
  591.0 18.0 %collective-permute-start.1 = (bf16[64,1536]{1,0:T(8,128)(2,1)}, bf16[64,1536]{1,0:T(8,128)(2,1)S(1)}, u32[]{:S(2)}, u32[]{:S(2)}) collective-permute-start(bf16[64,1536]{1,0:T(8,128)(2,1)} %get-tuple-element.1134), channel_id=1, source_target_pairs={{32,0},{64,32},{96,64},{128,96},{160,128},{192,160},{224,192},{0,2... | collective-permute-start | bytes 589832 | tf_op jit(solution)/shard_map/while/body/eval_jaxpr/ppermute | solution.py:16
  609.7 10.3 %collective-permute-start.1 = (bf16[64,1536]{1,0:T(8,128)(2,1)}, bf16[64,1536]{1,0:T(8,128)(2,1)S(1)}, u32[]{:S(2)}, u32[]{:S(2)}) collective-permute-start(bf16[64,1536]{1,0:T(8,128)(2,1)} %get-tuple-element.1134), channel_id=1, source_target_pairs={{32,0},{64,32},{96,64},{128,96},{160,128},{192,160},{224,192},{0,2... | collective-permute-start | bytes 589832 | tf_op jit(solution)/shard_map/while/body/eval_jaxpr/ppermute | solution.py:16
  620.7 10.9 %collective-permute-start.1 = (bf16[64,1536]{1,0:T(8,128)(2,1)}, bf16[64,1536]{1,0:T(8,128)(2,1)S(1)}, u32[]{:S(2)}, u32[]{:S(2)}) collective-permute-start(bf16[64,1536]{1,0:T(8,128)(2,1)} %get-tuple-element.1134), channel_id=1, source_target_pairs={{32,0},{64,32},{96,64},{128,96},{160,128},{192,160},{224,192},{0,2... | collective-permute-start | bytes 589832 | tf_op jit(solution)/shard_map/while/body/eval_jaxpr/ppermute | solution.py:16
  632.4 20.6 %collective-permute-start.1 = (bf16[64,1536]{1,0:T(8,128)(2,1)}, bf16[64,1536]{1,0:T(8,128)(2,1)S(1)}, u32[]{:S(2)}, u32[]{:S(2)}) collective-permute-start(bf16[64,1536]{1,0:T(8,128)(2,1)} %get-tuple-element.1134), channel_id=1, source_target_pairs={{32,0},{64,32},{96,64},{128,96},{160,128},{192,160},{224,192},{0,2... | collective-permute-start | bytes 589832 | tf_op jit(solution)/shard_map/while/body/eval_jaxpr/ppermute | solution.py:16
  664.8 9.9 %collective-permute-start.1 = (bf16[64,1536]{1,0:T(8,128)(2,1)}, bf16[64,1536]{1,0:T(8,128)(2,1)S(1)}, u32[]{:S(2)}, u32[]{:S(2)}) collective-permute-start(bf16[64,1536]{1,0:T(8,128)(2,1)} %get-tuple-element.1134), channel_id=1, source_target_pairs={{32,0},{64,32},{96,64},{128,96},{160,128},{192,160},{224,192},{0,2... | collective-permute-start | bytes 589832 | tf_op jit(solution)/shard_map/while/body/eval_jaxpr/ppermute | solution.py:16
  686.5 9.8 %collective-permute-start.1 = (bf16[64,1536]{1,0:T(8,128)(2,1)}, bf16[64,1536]{1,0:T(8,128)(2,1)S(1)}, u32[]{:S(2)}, u32[]{:S(2)}) collective-permute-start(bf16[64,1536]{1,0:T(8,128)(2,1)} %get-tuple-element.1134), channel_id=1, source_target_pairs={{32,0},{64,32},{96,64},{128,96},{160,128},{192,160},{224,192},{0,2... | collective-permute-start | bytes 589832 | tf_op jit(solution)/shard_map/while/body/eval_jaxpr/ppermute | solution.py:16
  708.1 10.3 %collective-permute-start.1 = (bf16[64,1536]{1,0:T(8,128)(2,1)}, bf16[64,1536]{1,0:T(8,128)(2,1)S(1)}, u32[]{:S(2)}, u32[]{:S(2)}) collective-permute-start(bf16[64,1536]{1,0:T(8,128)(2,1)} %get-tuple-element.1134), channel_id=1, source_target_pairs={{32,0},{64,32},{96,64},{128,96},{160,128},{192,160},{224,192},{0,2... | collective-permute-start | bytes 589832 | tf_op jit(solution)/shard_map/while/body/eval_jaxpr/ppermute | solution.py:16
  738.3 18.1 %collective-permute-start.1 = (bf16[64,1536]{1,0:T(8,128)(2,1)}, bf16[64,1536]{1,0:T(8,128)(2,1)S(1)}, u32[]{:S(2)}, u32[]{:S(2)}) collective-permute-start(bf16[64,1536]{1,0:T(8,128)(2,1)} %get-tuple-element.1134), channel_id=1, source_target_pairs={{32,0},{64,32},{96,64},{128,96},{160,128},{192,160},{224,192},{0,2... | collective-permute-start | bytes 589832 | tf_op jit(solution)/shard_map/while/body/eval_jaxpr/ppermute | solution.py:16
  766.1 14.9 %collective-permute-start.1 = (bf16[64,1536]{1,0:T(8,128)(2,1)}, bf16[64,1536]{1,0:T(8,128)(2,1)S(1)}, u32[]{:S(2)}, u32[]{:S(2)}) collective-permute-start(bf16[64,1536]{1,0:T(8,128)(2,1)} %get-tuple-element.1134), channel_id=1, source_target_pairs={{32,0},{64,32},{96,64},{128,96},{160,128},{192,160},{224,192},{0,2... | collective-permute-start | bytes 589832 | tf_op jit(solution)/shard_map/while/body/eval_jaxpr/ppermute | solution.py:16
  790.7 15.2 %collective-permute-start.1 = (bf16[64,1536]{1,0:T(8,128)(2,1)}, bf16[64,1536]{1,0:T(8,128)(2,1)S(1)}, u32[]{:S(2)}, u32[]{:S(2)}) collective-permute-start(bf16[64,1536]{1,0:T(8,128)(2,1)} %get-tuple-element.1134), channel_id=1, source_target_pairs={{32,0},{64,32},{96,64},{128,96},{160,128},{192,160},{224,192},{0,2... | collective-permute-start | bytes 589832 | tf_op jit(solution)/shard_map/while/body/eval_jaxpr/ppermute | solution.py:16
  806.6 20.9 %collective-permute-start.1 = (bf16[64,1536]{1,0:T(8,128)(2,1)}, bf16[64,1536]{1,0:T(8,128)(2,1)S(1)}, u32[]{:S(2)}, u32[]{:S(2)}) collective-permute-start(bf16[64,1536]{1,0:T(8,128)(2,1)} %get-tuple-element.1134), channel_id=1, source_target_pairs={{32,0},{64,32},{96,64},{128,96},{160,128},{192,160},{224,192},{0,2... | collective-permute-start | bytes 589832 | tf_op jit(solution)/shard_map/while/body/eval_jaxpr/ppermute | solution.py:16
  (53 other events, 142.8 us)
Sparse Core Ops, SparseCore 0:
  9.9 70.9 all-gather.2
  829.3 131.8 reduce-scatter.1
where the time goes:
time: 972 us; the launch traced here: 970 us
  waiting for transfers between devices  508 us (52%)
  starting transfers between devices  201 us (21%)
  matrix products  133 us (14%)
  other arithmetic  61.9 us (6%)
  local copies, waits for them, and re-layouts  50.3 us (5%)
  between operations  14.1 us (1%)
    ppermute x38, waiting for transfers between devices, from_behind(): return lax.ppermute(block, axis, route)  306 us
    ppermute x38, starting transfers between devices, from_behind(): return lax.ppermute(block, axis, route)  201 us
    reduce_scatter x1, waiting for transfers between devices, in_one_piece(): out = lax.psum_scatter(both, axis, scatter_dimension=dim, tiled=True)  132 us
    all_gather x1, waiting for transfers between devices, local(): layer_weight = lax.all_gather(frozen_weight[0], 'dp', axis=0, tiled=True)  68.9 us
    dot_general x8, matrix products, forward_layer_pass(): jnp.dot(normalized_hidden, layer_weight, preferred_element_type=jnp.float32)  32.5 us
    dot_general x8, matrix products, backward_layer_pass(): lax.dot_general(preactivation_gradient, layer_weight, (((1,), (1,)), ((),...  31.2 us
  transfers between devices with their start and end apart: 40, of which 40 were waited for; matrix products, arithmetic and copies ran while one was open for 0% of the time, Pallas kernels for 0%

commit v1 on v0

--- a/solution.py
+++ b/solution.py
@@ -124,7 +124,13 @@
 ):
     sections = lax.axis_size("section")
     position = lax.axis_index("section")
-    layer_weight = lax.all_gather(frozen_weight[0], "dp", axis=0, tiled=True)
+    my_data = frozen_weight[0]
+    ledger = []
+    for _ in range(lax.axis_size("dp")):
+        ledger.append(my_data)
+    r2 = jnp.stack(ledger)
+    field_out = lax.all_to_all(r2, "dp", 0, 0)
+    layer_weight = jnp.concatenate(field_out, axis=0)
     down_weight_rows = adapter_down_weight[0]
     up_weight_rows = adapter_up_weight[0]
     gain_row = layer_norm_gain[0]

time: 972 us -> 1020 us (1.049)
  waiting for transfers between devices: 508 us -> 543 us
    all_to_all x0 -> x1, waiting for transfers between devices: none -> 105 us  [local(): field_out = lax.all_to_all(r2, 'dp', 0, 0)]
    all_gather x1 -> x0, waiting for transfers between devices: 68.9 us -> none  [local(): layer_weight = lax.all_gather(frozen_weight[0], 'dp', axis=0, tiled=True)]
    another operation x28 -> x29, local copies, waits for them, and re-layouts: 17.4 us -> 21 us
where the time goes in v1:
time: 1020 us
  waiting for transfers between devices  543 us (53%)
  starting transfers between devices  210 us (21%)
  matrix products  132 us (13%)
  other arithmetic  61.7 us (6%)
  local copies, waits for them, and re-layouts  54.4 us (5%)
  between operations  14.1 us (1%)
    ppermute x38, waiting for transfers between devices, from_behind(): return lax.ppermute(block, axis, route)  306 us
    ppermute x38, starting transfers between devices, from_behind(): return lax.ppermute(block, axis, route)  200 us
    reduce_scatter x1, waiting for transfers between devices, in_one_piece(): out = lax.psum_scatter(both, axis, scatter_dimension=dim, tiled=True)  132 us
    all_to_all x1, waiting for transfers between devices, local(): field_out = lax.all_to_all(r2, 'dp', 0, 0)  105 us
    dot_general x8, matrix products, forward_layer_pass(): jnp.dot(normalized_hidden, layer_weight, preferred_element_type=jnp.float32)  32.8 us
    dot_general x8, matrix products, backward_layer_pass(): lax.dot_general(preactivation_gradient, layer_weight, (((1,), (1,)), ((),...  31.2 us
  transfers between devices with their start and end apart: 40, of which 40 were waited for; matrix products, arithmetic and copies ran while one was open for 0% of the time, Pallas kernels for 0%

profile of v1, /device:TPU:6, one launch (start us, length us, event | category | flops | bytes accessed | tf_op | source)
XLA Modules:
  0.0 1016.6 jit_solution(15272132870546261002)
XLA Ops:
  22.9 104.8 %all-to-all-done = bf16[32,48,1536]{2,1,0:T(8,128)(2,1)} async-done(((bf16[32,48,1536]{2,1,0:T(8,128)(2,1)}), bf16[32,48,1536]{2,1,0:T(8,128)(2,1)}, u32[]{:S(2)}, u32[]{:S(2)}) %all-to-all-start) | async-done | bytes 4718624 | tf_op jit(solution)/shard_map/all_to_all | solution.py:132
  133.7 397.6 %while.42 = (s32[]{:T(128)}, bf16[64,1536]{1,0:T(8,128)(2,1)}, bf16[2,4,64,1536]{3,2,1,0:T(8,128)(2,1)S(1)}, bf16[2,4,64,1536]{3,2,1,0:T(8,128)(2,1)}, bf16[2,4,...) while((s32[]{:T(128)}, bf16[64,1536]{1,0:T(8,128)(2,1)}, ...), condition=%wide.region_4.5_spmd, body=%wide.region_0.4_spmd.sunk | while | flops 332176448 | bytes 21725468 | solution.py:236
  144.6 11.8 %collective-permute-start = (bf16[64,1536]{1,0:T(8,128)(2,1)}, bf16[64,1536]{1,0:T(8,128)(2,1)S(1)}, u32[]{:S(2)}, u32[]{:S(2)}) collective-permute-start(bf16[64,1536]{1,0:T(8,128)(2,1)} %get-tuple-element.1111), channel_id=1, source_target_pairs={{224,0},{0,32},{32,64},{64,96},{96,128},{128,160},{160,192},{192,2... | collective-permute-start | bytes 589832 | tf_op jit(solution)/shard_map/while/body/eval_jaxpr/ppermute | solution.py:16
  161.3 19.1 %collective-permute-start = (bf16[64,1536]{1,0:T(8,128)(2,1)}, bf16[64,1536]{1,0:T(8,128)(2,1)S(1)}, u32[]{:S(2)}, u32[]{:S(2)}) collective-permute-start(bf16[64,1536]{1,0:T(8,128)(2,1)} %get-tuple-element.1111), channel_id=1, source_target_pairs={{224,0},{0,32},{32,64},{64,96},{96,128},{128,160},{160,192},{192,2... | collective-permute-start | bytes 589832 | tf_op jit(solution)/shard_map/while/body/eval_jaxpr/ppermute | solution.py:16
  185.3 19.1 %collective-permute-start = (bf16[64,1536]{1,0:T(8,128)(2,1)}, bf16[64,1536]{1,0:T(8,128)(2,1)S(1)}, u32[]{:S(2)}, u32[]{:S(2)}) collective-permute-start(bf16[64,1536]{1,0:T(8,128)(2,1)} %get-tuple-element.1111), channel_id=1, source_target_pairs={{224,0},{0,32},{32,64},{64,96},{96,128},{128,160},{160,192},{192,2... | collective-permute-start | bytes 589832 | tf_op jit(solution)/shard_map/while/body/eval_jaxpr/ppermute | solution.py:16
  209.3 19.1 %collective-permute-start = (bf16[64,1536]{1,0:T(8,128)(2,1)}, bf16[64,1536]{1,0:T(8,128)(2,1)S(1)}, u32[]{:S(2)}, u32[]{:S(2)}) collective-permute-start(bf16[64,1536]{1,0:T(8,128)(2,1)} %get-tuple-element.1111), channel_id=1, source_target_pairs={{224,0},{0,32},{32,64},{64,96},{96,128},{128,160},{160,192},{192,2... | collective-permute-start | bytes 589832 | tf_op jit(solution)/shard_map/while/body/eval_jaxpr/ppermute | solution.py:16
  239.3 15.9 %collective-permute-done = bf16[64,1536]{1,0:T(8,128)(2,1)S(1)} collective-permute-done((bf16[64,1536]{1,0:T(8,128)(2,1)}, bf16[64,1536]{1,0:T(8,128)(2,1)S(1)}, u32[]{:S(2)}, u32[]{:S(2)}) %collective-permute-start) | collective-permute-done | bytes 196640 | tf_op jit(solution)/shard_map/while/body/eval_jaxpr/ppermute | solution.py:16
  255.9 13.8 %conditional.4 = (bf16[64,1536]{1,0:T(8,128)(2,1)}, bf16[2,4,64,1536]{3,2,1,0:T(8,128)(2,1)S(1)}, bf16[2,4,64,1536]{3,2,1,0:T(8,128)(2,1)}, bf16[2,4,64,64]{3,2,...) conditional(s32[]{:T(128)} %convert_element_type.177, ...), branch_computations={%region_1.1_spmd, %region_2.3_spmd} | conditional | flops 332176448 | bytes 20152056 | solution.py:223
  279.3 13.8 %conditional.4 = (bf16[64,1536]{1,0:T(8,128)(2,1)}, bf16[2,4,64,1536]{3,2,1,0:T(8,128)(2,1)S(1)}, bf16[2,4,64,1536]{3,2,1,0:T(8,128)(2,1)}, bf16[2,4,64,64]{3,2,...) conditional(s32[]{:T(128)} %convert_element_type.177, ...), branch_computations={%region_1.1_spmd, %region_2.3_spmd} | conditional | flops 332176448 | bytes 20152056 | solution.py:223
  303.4 13.8 %conditional.4 = (bf16[64,1536]{1,0:T(8,128)(2,1)}, bf16[2,4,64,1536]{3,2,1,0:T(8,128)(2,1)S(1)}, bf16[2,4,64,1536]{3,2,1,0:T(8,128)(2,1)}, bf16[2,4,64,64]{3,2,...) conditional(s32[]{:T(128)} %convert_element_type.177, ...), branch_computations={%region_1.1_spmd, %region_2.3_spmd} | conditional | flops 332176448 | bytes 20152056 | solution.py:223
  327.1 13.8 %conditional.4 = (bf16[64,1536]{1,0:T(8,128)(2,1)}, bf16[2,4,64,1536]{3,2,1,0:T(8,128)(2,1)S(1)}, bf16[2,4,64,1536]{3,2,1,0:T(8,128)(2,1)}, bf16[2,4,64,64]{3,2,...) conditional(s32[]{:T(128)} %convert_element_type.177, ...), branch_computations={%region_1.1_spmd, %region_2.3_spmd} | conditional | flops 332176448 | bytes 20152056 | solution.py:223
  377.3 15.7 %collective-permute-start = (bf16[64,1536]{1,0:T(8,128)(2,1)}, bf16[64,1536]{1,0:T(8,128)(2,1)S(1)}, u32[]{:S(2)}, u32[]{:S(2)}) collective-permute-start(bf16[64,1536]{1,0:T(8,128)(2,1)} %get-tuple-element.1111), channel_id=1, source_target_pairs={{224,0},{0,32},{32,64},{64,96},{96,128},{128,160},{160,192},{192,2... | collective-permute-start | bytes 589832 | tf_op jit(solution)/shard_map/while/body/eval_jaxpr/ppermute | solution.py:16
  403.9 15.0 %collective-permute-done = bf16[64,1536]{1,0:T(8,128)(2,1)S(1)} collective-permute-done((bf16[64,1536]{1,0:T(8,128)(2,1)}, bf16[64,1536]{1,0:T(8,128)(2,1)S(1)}, u32[]{:S(2)}, u32[]{:S(2)}) %collective-permute-start) | collective-permute-done | bytes 196640 | tf_op jit(solution)/shard_map/while/body/eval_jaxpr/ppermute | solution.py:16
  419.6 13.9 %conditional.4 = (bf16[64,1536]{1,0:T(8,128)(2,1)}, bf16[2,4,64,1536]{3,2,1,0:T(8,128)(2,1)S(1)}, bf16[2,4,64,1536]{3,2,1,0:T(8,128)(2,1)}, bf16[2,4,64,64]{3,2,...) conditional(s32[]{:T(128)} %convert_element_type.177, ...), branch_computations={%region_1.1_spmd, %region_2.3_spmd} | conditional | flops 332176448 | bytes 20152056 | solution.py:223
  443.7 13.9 %conditional.4 = (bf16[64,1536]{1,0:T(8,128)(2,1)}, bf16[2,4,64,1536]{3,2,1,0:T(8,128)(2,1)S(1)}, bf16[2,4,64,1536]{3,2,1,0:T(8,128)(2,1)}, bf16[2,4,64,64]{3,2,...) conditional(s32[]{:T(128)} %convert_element_type.177, ...), branch_computations={%region_1.1_spmd, %region_2.3_spmd} | conditional | flops 332176448 | bytes 20152056 | solution.py:223
  467.6 13.9 %conditional.4 = (bf16[64,1536]{1,0:T(8,128)(2,1)}, bf16[2,4,64,1536]{3,2,1,0:T(8,128)(2,1)S(1)}, bf16[2,4,64,1536]{3,2,1,0:T(8,128)(2,1)}, bf16[2,4,64,64]{3,2,...) conditional(s32[]{:T(128)} %convert_element_type.177, ...), branch_computations={%region_1.1_spmd, %region_2.3_spmd} | conditional | flops 332176448 | bytes 20152056 | solution.py:223
  491.4 13.8 %conditional.4 = (bf16[64,1536]{1,0:T(8,128)(2,1)}, bf16[2,4,64,1536]{3,2,1,0:T(8,128)(2,1)S(1)}, bf16[2,4,64,1536]{3,2,1,0:T(8,128)(2,1)}, bf16[2,4,64,64]{3,2,...) conditional(s32[]{:T(128)} %convert_element_type.177, ...), branch_computations={%region_1.1_spmd, %region_2.3_spmd} | conditional | flops 332176448 | bytes 20152056 | solution.py:223
  514.8 12.2 %collective-permute-start = (bf16[64,1536]{1,0:T(8,128)(2,1)}, bf16[64,1536]{1,0:T(8,128)(2,1)S(1)}, u32[]{:S(2)}, u32[]{:S(2)}) collective-permute-start(bf16[64,1536]{1,0:T(8,128)(2,1)} %get-tuple-element.1111), channel_id=1, source_target_pairs={{224,0},{0,32},{32,64},{64,96},{96,128},{128,160},{160,192},{192,2... | collective-permute-start | bytes 589832 | tf_op jit(solution)/shard_map/while/body/eval_jaxpr/ppermute | solution.py:16
  532.6 341.8 %while.43 = (s32[]{:T(128)}, bf16[64,1536]{1,0:T(8,128)(2,1)S(1)}, f32[64,1536]{1,0:T(8,128)S(1)}, f32[64,1536]{1,0:T(8,128)S(1)}, s32[]{:T(128)}, /*index=5*/pr...) while((s32[]{:T(128)}, bf16[64,1536]{1,0:T(8,128)(2,1)S(1)}, ...), condition=%wide.region_10.11_spmd, body=%wide.region_5.10_spmd.sunk | while | flops 356265024 | bytes 13259635 | solution.py:295
  533.3 19.2 %collective-permute-done.1 = bf16[64,1536]{1,0:T(8,128)(2,1)S(1)} collective-permute-done((bf16[64,1536]{1,0:T(8,128)(2,1)}, bf16[64,1536]{1,0:T(8,128)(2,1)S(1)}, u32[]{:S(2)}, u32[]{:S(2)}) %collective-permute-start.1) | collective-permute-done | bytes 196640 | tf_op jit(solution)/shard_map/while/body/eval_jaxpr/ppermute | solution.py:16
  552.5 11.8 %conditional.5 = (bf16[64,1536]{1,0:T(8,128)(2,1)}, f32[64,1536]{1,0:T(8,128)S(1)}, f32[64,1536]{1,0:T(8,128)S(1)}) conditional(s32[]{:T(128)} %convert_element_type.179, (f32[64,1536]{1,0:T(8,128)S(1)}, f32[64,1536]{1,0:T(8,128)S(1)}) %tuple.93, (pred[]{:T(512)}, s32[]{:T(128)}, s32[]{:T(128)}, f32[4,64,1536]{2,1,0:T(8,128)S(1)}, ...), branch_computations={%region_6.6_spmd, %region_7.9_spmd} | conditional | flops 356265024 | bytes 12472761 | solution.py:286
  575.5 11.8 %conditional.5 = (bf16[64,1536]{1,0:T(8,128)(2,1)}, f32[64,1536]{1,0:T(8,128)S(1)}, f32[64,1536]{1,0:T(8,128)S(1)}) conditional(s32[]{:T(128)} %convert_element_type.179, (f32[64,1536]{1,0:T(8,128)S(1)}, f32[64,1536]{1,0:T(8,128)S(1)}) %tuple.93, (pred[]{:T(512)}, s32[]{:T(128)}, s32[]{:T(128)}, f32[4,64,1536]{2,1,0:T(8,128)S(1)}, ...), branch_computations={%region_6.6_spmd, %region_7.9_spmd} | conditional | flops 356265024 | bytes 12472761 | solution.py:286
  619.8 11.8 %conditional.5 = (bf16[64,1536]{1,0:T(8,128)(2,1)}, f32[64,1536]{1,0:T(8,128)S(1)}, f32[64,1536]{1,0:T(8,128)S(1)}) conditional(s32[]{:T(128)} %convert_element_type.179, (f32[64,1536]{1,0:T(8,128)S(1)}, f32[64,1536]{1,0:T(8,128)S(1)}) %tuple.93, (pred[]{:T(512)}, s32[]{:T(128)}, s32[]{:T(128)}, f32[4,64,1536]{2,1,0:T(8,128)S(1)}, ...), branch_computations={%region_6.6_spmd, %region_7.9_spmd} | conditional | flops 356265024 | bytes 12472761 | solution.py:286
  640.0 12.1 %collective-permute-start.1 = (bf16[64,1536]{1,0:T(8,128)(2,1)}, bf16[64,1536]{1,0:T(8,128)(2,1)S(1)}, u32[]{:S(2)}, u32[]{:S(2)}) collective-permute-start(bf16[64,1536]{1,0:T(8,128)(2,1)} %get-tuple-element.1134), channel_id=1, source_target_pairs={{32,0},{64,32},{96,64},{128,96},{160,128},{192,160},{224,192},{0,2... | collective-permute-start | bytes 589832 | tf_op jit(solution)/shard_map/while/body/eval_jaxpr/ppermute | solution.py:16
  686.8 13.9 %collective-permute-done.1 = bf16[64,1536]{1,0:T(8,128)(2,1)S(1)} collective-permute-done((bf16[64,1536]{1,0:T(8,128)(2,1)}, bf16[64,1536]{1,0:T(8,128)(2,1)S(1)}, u32[]{:S(2)}, u32[]{:S(2)}) %collective-permute-start.1) | collective-permute-done | bytes 196640 | tf_op jit(solution)/shard_map/while/body/eval_jaxpr/ppermute | solution.py:16
  700.7 11.8 %conditional.5 = (bf16[64,1536]{1,0:T(8,128)(2,1)}, f32[64,1536]{1,0:T(8,128)S(1)}, f32[64,1536]{1,0:T(8,128)S(1)}) conditional(s32[]{:T(128)} %convert_element_type.179, (f32[64,1536]{1,0:T(8,128)S(1)}, f32[64,1536]{1,0:T(8,128)S(1)}) %tuple.93, (pred[]{:T(512)}, s32[]{:T(128)}, s32[]{:T(128)}, f32[4,64,1536]{2,1,0:T(8,128)S(1)}, ...), branch_computations={%region_6.6_spmd, %region_7.9_spmd} | conditional | flops 356265024 | bytes 12472761 | solution.py:286
  722.1 11.8 %conditional.5 = (bf16[64,1536]{1,0:T(8,128)(2,1)}, f32[64,1536]{1,0:T(8,128)S(1)}, f32[64,1536]{1,0:T(8,128)S(1)}) conditional(s32[]{:T(128)} %convert_element_type.179, (f32[64,1536]{1,0:T(8,128)S(1)}, f32[64,1536]{1,0:T(8,128)S(1)}) %tuple.93, (pred[]{:T(512)}, s32[]{:T(128)}, s32[]{:T(128)}, f32[4,64,1536]{2,1,0:T(8,128)S(1)}, ...), branch_computations={%region_6.6_spmd, %region_7.9_spmd} | conditional | flops 356265024 | bytes 12472761 | solution.py:286
  743.4 11.8 %conditional.5 = (bf16[64,1536]{1,0:T(8,128)(2,1)}, f32[64,1536]{1,0:T(8,128)S(1)}, f32[64,1536]{1,0:T(8,128)S(1)}) conditional(s32[]{:T(128)} %convert_element_type.179, (f32[64,1536]{1,0:T(8,128)S(1)}, f32[64,1536]{1,0:T(8,128)S(1)}) %tuple.93, (pred[]{:T(512)}, s32[]{:T(128)}, s32[]{:T(128)}, f32[4,64,1536]{2,1,0:T(8,128)S(1)}, ...), branch_computations={%region_6.6_spmd, %region_7.9_spmd} | conditional | flops 356265024 | bytes 12472761 | solution.py:286
  764.7 11.8 %conditional.5 = (bf16[64,1536]{1,0:T(8,128)(2,1)}, f32[64,1536]{1,0:T(8,128)S(1)}, f32[64,1536]{1,0:T(8,128)S(1)}) conditional(s32[]{:T(128)} %convert_element_type.179, (f32[64,1536]{1,0:T(8,128)S(1)}, f32[64,1536]{1,0:T(8,128)S(1)}) %tuple.93, (pred[]{:T(512)}, s32[]{:T(128)}, s32[]{:T(128)}, f32[4,64,1536]{2,1,0:T(8,128)S(1)}, ...), branch_computations={%region_6.6_spmd, %region_7.9_spmd} | conditional | flops 356265024 | bytes 12472761 | solution.py:286
  784.8 12.3 %collective-permute-start.1 = (bf16[64,1536]{1,0:T(8,128)(2,1)}, bf16[64,1536]{1,0:T(8,128)(2,1)S(1)}, u32[]{:S(2)}, u32[]{:S(2)}) collective-permute-start(bf16[64,1536]{1,0:T(8,128)(2,1)} %get-tuple-element.1134), channel_id=1, source_target_pairs={{32,0},{64,32},{96,64},{128,96},{160,128},{192,160},{224,192},{0,2... | collective-permute-start | bytes 589832 | tf_op jit(solution)/shard_map/while/body/eval_jaxpr/ppermute | solution.py:16
  853.8 20.6 %collective-permute-done.1 = bf16[64,1536]{1,0:T(8,128)(2,1)S(1)} collective-permute-done((bf16[64,1536]{1,0:T(8,128)(2,1)}, bf16[64,1536]{1,0:T(8,128)(2,1)S(1)}, u32[]{:S(2)}, u32[]{:S(2)}) %collective-permute-start.1) | collective-permute-done | bytes 196640 | tf_op jit(solution)/shard_map/while/body/eval_jaxpr/ppermute | solution.py:16
  876.1 132.1 %reduce-scatter.2.cloned.1.call-done = f32[128,48]{0,1:T(8,128)} async-done(((f32[128,1536]{0,1:T(8,128)}), f32[128,48]{0,1:T(8,128)}) %reduce-scatter.2.cloned.1.call-update) | async-done | bytes 24592 | tf_op jit(solution)/shard_map/reduce_scatter | solution.py:22
  (427 shorter events, 585.0 us)
Async XLA Ops:
  10.9 116.8 %all-to-all-start = ((bf16[32,48,1536]{2,1,0:T(8,128)(2,1)}), bf16[32,48,1536]{2,1,0:T(8,128)(2,1)}, u32[]{:S(2)}, u32[]{:S(2)}) async-start(bf16[32,48,1536]{2,1,0:T(8,128)(2,1)} %stack.3), calls=%async_computation | async-start | bytes 9437184 | tf_op jit(solution)/shard_map/all_to_all | solution.py:132
  21.0 987.3 %reduce-scatter.2.cloned.1.call-start = ((), (), s32[]{:S(2)}) async-start(), calls=%async_computation.2 | async-start | bytes 811008 | tf_op jit(solution)/shard_map/reduce_scatter | solution.py:22
  144.6 15.3 %collective-permute-start = (bf16[64,1536]{1,0:T(8,128)(2,1)}, bf16[64,1536]{1,0:T(8,128)(2,1)S(1)}, u32[]{:S(2)}, u32[]{:S(2)}) collective-permute-start(bf16[64,1536]{1,0:T(8,128)(2,1)} %get-tuple-element.1111), channel_id=1, source_target_pairs={{224,0},{0,32},{32,64},{64,96},{96,128},{128,160},{160,192},{192,2... | collective-permute-start | bytes 589832 | tf_op jit(solution)/shard_map/while/body/eval_jaxpr/ppermute | solution.py:16
  161.3 22.6 %collective-permute-start = (bf16[64,1536]{1,0:T(8,128)(2,1)}, bf16[64,1536]{1,0:T(8,128)(2,1)S(1)}, u32[]{:S(2)}, u32[]{:S(2)}) collective-permute-start(bf16[64,1536]{1,0:T(8,128)(2,1)} %get-tuple-element.1111), channel_id=1, source_target_pairs={{224,0},{0,32},{32,64},{64,96},{96,128},{128,160},{160,192},{192,2... | collective-permute-start | bytes 589832 | tf_op jit(solution)/shard_map/while/body/eval_jaxpr/ppermute | solution.py:16
  185.3 22.6 %collective-permute-start = (bf16[64,1536]{1,0:T(8,128)(2,1)}, bf16[64,1536]{1,0:T(8,128)(2,1)S(1)}, u32[]{:S(2)}, u32[]{:S(2)}) collective-permute-start(bf16[64,1536]{1,0:T(8,128)(2,1)} %get-tuple-element.1111), channel_id=1, source_target_pairs={{224,0},{0,32},{32,64},{64,96},{96,128},{128,160},{160,192},{192,2... | collective-permute-start | bytes 589832 | tf_op jit(solution)/shard_map/while/body/eval_jaxpr/ppermute | solution.py:16
  209.3 22.6 %collective-permute-start = (bf16[64,1536]{1,0:T(8,128)(2,1)}, bf16[64,1536]{1,0:T(8,128)(2,1)S(1)}, u32[]{:S(2)}, u32[]{:S(2)}) collective-permute-start(bf16[64,1536]{1,0:T(8,128)(2,1)} %get-tuple-element.1111), channel_id=1, source_target_pairs={{224,0},{0,32},{32,64},{64,96},{96,128},{128,160},{160,192},{192,2... | collective-permute-start | bytes 589832 | tf_op jit(solution)/shard_map/while/body/eval_jaxpr/ppermute | solution.py:16
  233.3 21.9 %collective-permute-start = (bf16[64,1536]{1,0:T(8,128)(2,1)}, bf16[64,1536]{1,0:T(8,128)(2,1)S(1)}, u32[]{:S(2)}, u32[]{:S(2)}) collective-permute-start(bf16[64,1536]{1,0:T(8,128)(2,1)} %get-tuple-element.1111), channel_id=1, source_target_pairs={{224,0},{0,32},{32,64},{64,96},{96,128},{128,160},{160,192},{192,2... | collective-permute-start | bytes 589832 | tf_op jit(solution)/shard_map/while/body/eval_jaxpr/ppermute | solution.py:16
  293.1 9.6 collective-permute-start
  317.2 9.2 collective-permute-start
  340.9 9.0 collective-permute-start
  351.2 15.0 %collective-permute-start = (bf16[64,1536]{1,0:T(8,128)(2,1)}, bf16[64,1536]{1,0:T(8,128)(2,1)S(1)}, u32[]{:S(2)}, u32[]{:S(2)}) collective-permute-start(bf16[64,1536]{1,0:T(8,128)(2,1)} %get-tuple-element.1111), channel_id=1, source_target_pairs={{224,0},{0,32},{32,64},{64,96},{96,128},{128,160},{160,192},{192,2... | collective-permute-start | bytes 589832 | tf_op jit(solution)/shard_map/while/body/eval_jaxpr/ppermute | solution.py:16
  377.3 19.2 %collective-permute-start = (bf16[64,1536]{1,0:T(8,128)(2,1)}, bf16[64,1536]{1,0:T(8,128)(2,1)S(1)}, u32[]{:S(2)}, u32[]{:S(2)}) collective-permute-start(bf16[64,1536]{1,0:T(8,128)(2,1)} %get-tuple-element.1111), channel_id=1, source_target_pairs={{224,0},{0,32},{32,64},{64,96},{96,128},{128,160},{160,192},{192,2... | collective-permute-start | bytes 589832 | tf_op jit(solution)/shard_map/while/body/eval_jaxpr/ppermute | solution.py:16
  397.9 21.0 %collective-permute-start = (bf16[64,1536]{1,0:T(8,128)(2,1)}, bf16[64,1536]{1,0:T(8,128)(2,1)S(1)}, u32[]{:S(2)}, u32[]{:S(2)}) collective-permute-start(bf16[64,1536]{1,0:T(8,128)(2,1)} %get-tuple-element.1111), channel_id=1, source_target_pairs={{224,0},{0,32},{32,64},{64,96},{96,128},{128,160},{160,192},{192,2... | collective-permute-start | bytes 589832 | tf_op jit(solution)/shard_map/while/body/eval_jaxpr/ppermute | solution.py:16
  433.4 9.6 collective-permute-start
  457.6 9.4 collective-permute-start
  481.5 9.2 collective-permute-start
  514.8 15.7 %collective-permute-start = (bf16[64,1536]{1,0:T(8,128)(2,1)}, bf16[64,1536]{1,0:T(8,128)(2,1)S(1)}, u32[]{:S(2)}, u32[]{:S(2)}) collective-permute-start(bf16[64,1536]{1,0:T(8,128)(2,1)} %get-tuple-element.1111), channel_id=1, source_target_pairs={{224,0},{0,32},{32,64},{64,96},{96,128},{128,160},{160,192},{192,2... | collective-permute-start | bytes 589832 | tf_op jit(solution)/shard_map/while/body/eval_jaxpr/ppermute | solution.py:16
  533.3 19.2 %collective-permute-start.1 = (bf16[64,1536]{1,0:T(8,128)(2,1)}, bf16[64,1536]{1,0:T(8,128)(2,1)S(1)}, u32[]{:S(2)}, u32[]{:S(2)}) collective-permute-start(bf16[64,1536]{1,0:T(8,128)(2,1)} %get-tuple-element.1134), channel_id=1, source_target_pairs={{32,0},{64,32},{96,64},{128,96},{160,128},{192,160},{224,192},{0,2... | collective-permute-start | bytes 589832 | tf_op jit(solution)/shard_map/while/body/eval_jaxpr/ppermute | solution.py:16
  564.2 11.3 %collective-permute-start.1 = (bf16[64,1536]{1,0:T(8,128)(2,1)}, bf16[64,1536]{1,0:T(8,128)(2,1)S(1)}, u32[]{:S(2)}, u32[]{:S(2)}) collective-permute-start(bf16[64,1536]{1,0:T(8,128)(2,1)} %get-tuple-element.1134), channel_id=1, source_target_pairs={{32,0},{64,32},{96,64},{128,96},{160,128},{192,160},{224,192},{0,2... | collective-permute-start | bytes 589832 | tf_op jit(solution)/shard_map/while/body/eval_jaxpr/ppermute | solution.py:16
  587.3 11.5 %collective-permute-start.1 = (bf16[64,1536]{1,0:T(8,128)(2,1)}, bf16[64,1536]{1,0:T(8,128)(2,1)S(1)}, u32[]{:S(2)}, u32[]{:S(2)}) collective-permute-start(bf16[64,1536]{1,0:T(8,128)(2,1)} %get-tuple-element.1134), channel_id=1, source_target_pairs={{32,0},{64,32},{96,64},{128,96},{160,128},{192,160},{224,192},{0,2... | collective-permute-start | bytes 589832 | tf_op jit(solution)/shard_map/while/body/eval_jaxpr/ppermute | solution.py:16
  610.5 9.3 collective-permute-start.1
  640.0 17.6 %collective-permute-start.1 = (bf16[64,1536]{1,0:T(8,128)(2,1)}, bf16[64,1536]{1,0:T(8,128)(2,1)S(1)}, u32[]{:S(2)}, u32[]{:S(2)}) collective-permute-start(bf16[64,1536]{1,0:T(8,128)(2,1)} %get-tuple-element.1134), channel_id=1, source_target_pairs={{32,0},{64,32},{96,64},{128,96},{160,128},{192,160},{224,192},{0,2... | collective-permute-start | bytes 589832 | tf_op jit(solution)/shard_map/while/body/eval_jaxpr/ppermute | solution.py:16
  658.3 9.5 collective-permute-start.1
  668.5 12.5 %collective-permute-start.1 = (bf16[64,1536]{1,0:T(8,128)(2,1)}, bf16[64,1536]{1,0:T(8,128)(2,1)S(1)}, u32[]{:S(2)}, u32[]{:S(2)}) collective-permute-start(bf16[64,1536]{1,0:T(8,128)(2,1)} %get-tuple-element.1134), channel_id=1, source_target_pairs={{32,0},{64,32},{96,64},{128,96},{160,128},{192,160},{224,192},{0,2... | collective-permute-start | bytes 589832 | tf_op jit(solution)/shard_map/while/body/eval_jaxpr/ppermute | solution.py:16
  681.7 19.1 %collective-permute-start.1 = (bf16[64,1536]{1,0:T(8,128)(2,1)}, bf16[64,1536]{1,0:T(8,128)(2,1)S(1)}, u32[]{:S(2)}, u32[]{:S(2)}) collective-permute-start(bf16[64,1536]{1,0:T(8,128)(2,1)} %get-tuple-element.1134), channel_id=1, source_target_pairs={{32,0},{64,32},{96,64},{128,96},{160,128},{192,160},{224,192},{0,2... | collective-permute-start | bytes 589832 | tf_op jit(solution)/shard_map/while/body/eval_jaxpr/ppermute | solution.py:16
  712.5 9.6 collective-permute-start.1
  733.8 9.6 collective-permute-start.1
  755.2 9.6 collective-permute-start.1
  784.8 17.3 %collective-permute-start.1 = (bf16[64,1536]{1,0:T(8,128)(2,1)}, bf16[64,1536]{1,0:T(8,128)(2,1)S(1)}, u32[]{:S(2)}, u32[]{:S(2)}) collective-permute-start(bf16[64,1536]{1,0:T(8,128)(2,1)} %get-tuple-element.1134), channel_id=1, source_target_pairs={{32,0},{64,32},{96,64},{128,96},{160,128},{192,160},{224,192},{0,2... | collective-permute-start | bytes 589832 | tf_op jit(solution)/shard_map/while/body/eval_jaxpr/ppermute | solution.py:16
  811.8 14.9 %collective-permute-start.1 = (bf16[64,1536]{1,0:T(8,128)(2,1)}, bf16[64,1536]{1,0:T(8,128)(2,1)S(1)}, u32[]{:S(2)}, u32[]{:S(2)}) collective-permute-start(bf16[64,1536]{1,0:T(8,128)(2,1)} %get-tuple-element.1134), channel_id=1, source_target_pairs={{32,0},{64,32},{96,64},{128,96},{160,128},{192,160},{224,192},{0,2... | collective-permute-start | bytes 589832 | tf_op jit(solution)/shard_map/while/body/eval_jaxpr/ppermute | solution.py:16
  836.3 16.7 %collective-permute-start.1 = (bf16[64,1536]{1,0:T(8,128)(2,1)}, bf16[64,1536]{1,0:T(8,128)(2,1)S(1)}, u32[]{:S(2)}, u32[]{:S(2)}) collective-permute-start(bf16[64,1536]{1,0:T(8,128)(2,1)} %get-tuple-element.1134), channel_id=1, source_target_pairs={{32,0},{64,32},{96,64},{128,96},{160,128},{192,160},{224,192},{0,2... | collective-permute-start | bytes 589832 | tf_op jit(solution)/shard_map/while/body/eval_jaxpr/ppermute | solution.py:16
  853.7 20.7 %collective-permute-start.1 = (bf16[64,1536]{1,0:T(8,128)(2,1)}, bf16[64,1536]{1,0:T(8,128)(2,1)S(1)}, u32[]{:S(2)}, u32[]{:S(2)}) collective-permute-start(bf16[64,1536]{1,0:T(8,128)(2,1)} %get-tuple-element.1134), channel_id=1, source_target_pairs={{32,0},{64,32},{96,64},{128,96},{160,128},{192,160},{224,192},{0,2... | collective-permute-start | bytes 589832 | tf_op jit(solution)/shard_map/while/body/eval_jaxpr/ppermute | solution.py:16
  (57 other events, 197.9 us)
Sparse Core Ops, SparseCore 0:
  876.3 131.9 reduce-scatter.1
